TPU v7x, 32 devices: a whole 2x2x4 slice. The times are simulated.
32 devices in a mesh: pairs: 8 (over z, y), dom: 4 (over x, core).
Axes of the slice: x: 2, y: 2, z: 4, core: 2. Of those that a mesh axis runs over, the one named last changes fastest.
Arguments:
- amplitude: bfloat16 [64, 384, 384], P('pairs', 'dom'), may hold values from -2 to 2
- integrals: bfloat16 [64, 384, 384], P('pairs', 'dom'), may hold values from -6 to 6
- virtual_energy: float32 [64, 384], P('pairs'), may hold values from 0.2 to 1.5
- occupied_gap: float32 [64], P('pairs'), may hold values from 0.3 to 1.5
- pair_slot: int32 [64], replicated, may hold values from 0 to 63, as said below
- coupling_source: int32 [128], replicated, may hold values from 0 to 63, as said below
- coupling_target: int32 [128], replicated, may hold values from 0 to 63, as said below
- coupling_fock: float32 [128], P(('pairs', 'dom')), may hold values from -3 to 3
- coupling_intersection: bfloat16 [128, 384, 384], P(('pairs', 'dom')), may hold values from -0.3125 to 0.3125
Outputs:
- updated_amplitude: float32 [64, 384, 384], P('pairs', 'dom')
- residual: float32 [64, 384, 384], P('pairs', 'dom')
Inputs may be any that keep to these rules, and one draw needn't show every extreme that they name: A permutation: pair p is stored at position pair_slot[p], which lies on index pair_slot[p] // 8 of pairs. `coupling_target`: coupling c is held by index c // 16 of pairs, and its target pair is stored on that same index; the two couplings that share a source pair on one holder have different targets. `coupling_source`: among the 16 couplings of one holder, every source pair appears in exactly two, and there are 8 distinct source pairs; of the pairs stored on any one index of pairs, a holder uses at most 2 distinct ones as sources, and exactly 2 for some indices on every holder.
All inputs are finite; a program needn't handle non-finite values.
Results may differ from a plain program's by a relative error of at most 0.0024.
Values may be sent and summed in bfloat16 or wider, within the bound.
A program may use at most 128 MiB of HBM per device.

v0:
```python
import functools

import jax
import jax.numpy as jnp
from jax import lax
from jax.experimental import pallas as pl
from jax.experimental.pallas import tpu as pltpu
from jax.sharding import PartitionSpec as P

SRC_CAP = 2
CHUNK_ROWS = 16
MESH = pl.DeviceIdType.MESH
VMEM = pltpu.VMEM
SMEM = pltpu.SMEM


def exchange_kernel(
    holders,
    quarters,
    slot_ref,
    source_ref,
    target_ref,
    fock_ref,
    amp_hbm,
    inter_hbm,
    terms_ref,
    local_ref,
    out_ref,
    inter_ref,
    held_ref,
    inter_sem,
    amp_ref,
    amp_sem,
    whole,
    picked,
    sent_terms,
    send1,
    recv1,
    local1,
    send2,
    recv2,
    send3,
    recv3,
    local3,
    inter_x,
    fock_out,
    fock_in,
    half_terms,
    swap_send,
    swap_recv,
    half_send,
    half_recv,
    half_local,
    *arrived,
):
    amp_copy = pltpu.make_async_copy(amp_hbm, amp_ref, amp_sem)
    amp_copy.start()
    me = lax.axis_index("pairs")
    quarter = lax.axis_index("dom")
    chunks = len(arrived)
    slots, chunk_rows, width = arrived[0].shape
    rows = chunk_rows * chunks
    group = inter_hbm.shape[0]
    half = holders // 2
    my_half = me // half
    in_half = me % half

    extra = whole.shape[0] - group
    full = group - extra
    partner = (quarter + quarters // 2) % quarters
    sibling = quarter + 1 - 2 * (quarter % 2)

    barrier = pltpu.get_barrier_semaphore()

    def greet(j, carry):
        pl.semaphore_signal(
            barrier, inc=1, device_id=((me + j) % holders, quarter), device_id_type=MESH
        )
        return carry

    lax.fori_loop(1, holders, greet, 0)
    for d in range(1, quarters):
        pl.semaphore_signal(
            barrier, inc=1, device_id=(me, (quarter + d) % quarters), device_id_type=MESH
        )

    def inter_copy(c):
        return pltpu.make_async_copy(inter_hbm.at[c], inter_ref.at[c], inter_sem.at[c])

    def fetch(c, carry):
        inter_copy(c).start()
        return carry

    lax.fori_loop(0, group, fetch, 0)

    pair_count = amp_ref.shape[0]
    couplings = source_ref.shape[0] // holders
    base = me * pair_count
    unroll = 8 if couplings % 8 == 0 else 1

    def holder_step(h, carry):
        def block(i, ab):
            first, second = ab
            for u in range(unroll):
                local = slot_ref[source_ref[h * couplings + i * unroll + u]] - base
                mine = (local >= 0) & (local < pair_count)
                free = first < 0
                second = jnp.where(mine & jnp.logical_not(free) & (local != first), local, second)
                first = jnp.where(mine & free, local, first)
            return first, second

        first, second = lax.fori_loop(
            0, couplings // unroll, block, (jnp.int32(-1), jnp.int32(-1))
        )
        out_ref[h * SRC_CAP] = amp_ref[jnp.maximum(first, 0)]
        out_ref[h * SRC_CAP + 1] = amp_ref[jnp.maximum(second, 0)]
        return carry

    fock_out[...] = jnp.full(fock_out.shape, fock_ref[group - 1], jnp.float32)
    amp_copy.wait()
    lax.fori_loop(0, holders, holder_step, 0)
    pl.semaphore_wait(barrier, holders - 1 + quarters - 1)

    def swaps():
        for i, (src, dst) in enumerate(((inter_hbm.at[group - 1], inter_x), (fock_out, fock_in))):
            yield pltpu.make_async_remote_copy(
                src_ref=src,
                dst_ref=dst,
                send_sem=swap_send.at[i],
                recv_sem=swap_recv.at[i],
                device_id=(me, partner),
                device_id_type=MESH,
            )

    if extra:
        for copy in swaps():
            copy.start()

    def owner_copy(k, h):
        span = pl.ds(k * chunk_rows, chunk_rows)
        return pltpu.make_async_remote_copy(
            src_ref=out_ref.at[pl.ds(h * SRC_CAP, SRC_CAP), span],
            dst_ref=arrived[k].at[pl.ds(me * SRC_CAP, SRC_CAP)],
            send_sem=send1.at[k, h],
            recv_sem=recv1.at[k, me],
            device_id=(h, quarter),
            device_id_type=MESH,
        )

    def arrival(k, h):
        span = pl.ds(k * chunk_rows, chunk_rows)
        return pltpu.make_async_remote_copy(
            src_ref=out_ref.at[pl.ds(h * SRC_CAP, SRC_CAP), span],
            dst_ref=arrived[k].at[pl.ds(h * SRC_CAP, SRC_CAP)],
            send_sem=send1.at[k, h],
            recv_sem=recv1.at[k, h],
            device_id=(h, quarter),
            device_id_type=MESH,
        )

    def own_copy(k):
        span = pl.ds(k * chunk_rows, chunk_rows)
        return pltpu.make_async_copy(
            out_ref.at[pl.ds(me * SRC_CAP, SRC_CAP), span],
            arrived[k].at[pl.ds(me * SRC_CAP, SRC_CAP)],
            local1.at[k],
        )

    for k in range(chunks):

        def far(j, carry, k=k):
            owner_copy(k, (1 - my_half) * half + (in_half + j) % half).start()
            return carry

        def near(j, carry, k=k):
            owner_copy(k, my_half * half + (in_half + j) % half).start()
            return carry

        lax.fori_loop(0, half, far, 0)
        lax.fori_loop(1, half, near, 0)
        own_copy(k).start()

    def own_step(c, carry):
        slot = slot_ref[source_ref[me * couplings + c]]
        owner = lax.div(slot, jnp.int32(pair_count))

        def block(i, first):
            for u in range(unroll):
                at = couplings - 1 - (i * unroll + u)
                other = slot_ref[source_ref[me * couplings + at]]
                same = lax.div(other, jnp.int32(pair_count)) == owner
                first = jnp.where(same, other, first)
            return first

        first = lax.fori_loop(0, couplings // unroll, block, slot)
        held_ref[c] = owner * SRC_CAP + jnp.where(first == slot, 0, 1)
        local_ref[c] = slot_ref[target_ref[me * couplings + c]] - base
        return carry

    lax.fori_loop(0, couplings, own_step, 0)

    def peer_copy(k, d):
        peer = (quarter + d) % quarters
        return pltpu.make_async_remote_copy(
            src_ref=picked.at[d - 1, k],
            dst_ref=whole.at[:, pl.ds(pl.multiple_of(quarter * rows + k * chunk_rows, 16), chunk_rows)],
            send_sem=send2.at[k, d],
            recv_sem=recv2.at[k, d],
            device_id=(me, peer),
            device_id_type=MESH,
        )

    def peer_arrival(k, d):
        peer = (quarter + quarters - d) % quarters
        return pltpu.make_async_remote_copy(
            src_ref=picked.at[d - 1, k],
            dst_ref=whole.at[:, pl.ds(pl.multiple_of(peer * rows + k * chunk_rows, 16), chunk_rows)],
            send_sem=send2.at[k, d],
            recv_sem=recv2.at[k, d],
            device_id=(me, peer),
            device_id_type=MESH,
        )

    for k in range(chunks):

        def take(j, carry, k=k):
            arrival(k, (me + j) % holders).wait_recv()
            return carry

        lax.fori_loop(1, holders, take, 0)
        own_copy(k).wait()
        picked_all = []
        for d in sorted(range(1, quarters), key=lambda d: abs(2 * d - quarters)):
            peer = (quarter + d) % quarters

            def pick(c, carry, k=k, d=d, peer=peer):
                picked[d - 1, k, c] = arrived[k][held_ref[peer * group + c]]
                return carry

            lax.fori_loop(0, group, pick, 0)
            if extra:
                last = ((peer + quarters // 2) % quarters) * group + group - 1
                picked[d - 1, k, group] = arrived[k][held_ref[last]]
            picked_all.append(d)
            if len(picked_all) == quarters - 1:
                for e in picked_all:
                    peer_copy(k, e).start()

        def keep(c, carry, k=k):
            start = pl.multiple_of(quarter * rows + k * chunk_rows, 16)
            whole[c, pl.ds(start, chunk_rows)] = arrived[k][held_ref[quarter * group + c]]
            return carry

        lax.fori_loop(0, group, keep, 0)
        if extra:
            start = pl.multiple_of(quarter * rows + k * chunk_rows, 16)
            last = partner * group + group - 1
            whole[group, pl.ds(start, chunk_rows)] = arrived[k][held_ref[last]]

    for k in range(chunks):
        for d in range(1, quarters):
            peer_arrival(k, d).wait_recv()

    def term_copy(c, d):
        peer = (quarter + d) % quarters
        return pltpu.make_async_remote_copy(
            src_ref=sent_terms.at[c, pl.ds(pl.multiple_of(peer * rows, 16), rows)],
            dst_ref=terms_ref.at[quarter * group + c],
            send_sem=send3.at[c, d],
            recv_sem=recv3.at[c, d],
            device_id=(me, peer),
            device_id_type=MESH,
        )

    def term_arrival(c, d):
        peer = (quarter + quarters - d) % quarters
        return pltpu.make_async_remote_copy(
            src_ref=sent_terms.at[c, pl.ds(pl.multiple_of(peer * rows, 16), rows)],
            dst_ref=terms_ref.at[peer * group + c],
            send_sem=send3.at[c, d],
            recv_sem=recv3.at[c, d],
            device_id=(me, peer),
            device_id_type=MESH,
        )

    def own_term(c):
        return pltpu.make_async_copy(
            sent_terms.at[c, pl.ds(pl.multiple_of(quarter * rows, 16), rows)],
            terms_ref.at[quarter * group + c],
            local3.at[c],
        )

    def multiply(c, carry):
        inter_copy(c).wait()
        inter = inter_ref[c]
        left = jnp.dot(inter, whole[c], preferred_element_type=jnp.float32).astype(jnp.bfloat16)
        projected = lax.dot_general(
            left, inter, (((1,), (1,)), ((), ())), preferred_element_type=jnp.float32
        )
        sent_terms[c] = (fock_ref[c] * projected).astype(jnp.bfloat16)
        for d in range(1, quarters):
            term_copy(c, d).start()
        own_term(c).start()
        return carry

    lax.fori_loop(0, full, multiply, 0)

    def half_copy(i):
        return pltpu.make_async_remote_copy(
            src_ref=half_terms.at[i, pl.ds(pl.multiple_of((sibling % 2) * rows, 16), rows)],
            dst_ref=terms_ref.at[(quarter, partner)[i] * group + group - 1],
            send_sem=half_send.at[i],
            recv_sem=half_recv.at[i],
            device_id=(me, sibling),
            device_id_type=MESH,
        )

    def half_arrival(i):
        owner = (sibling, (sibling + quarters // 2) % quarters)[i]
        return pltpu.make_async_remote_copy(
            src_ref=half_terms.at[i, pl.ds(pl.multiple_of((sibling % 2) * rows, 16), rows)],
            dst_ref=terms_ref.at[owner * group + group - 1],
            send_sem=half_send.at[i],
            recv_sem=half_recv.at[i],
            device_id=(me, sibling),
            device_id_type=MESH,
        )

    def half_own(i):
        return pltpu.make_async_copy(
            half_terms.at[i, pl.ds(pl.multiple_of((quarter % 2) * rows, 16), rows)],
            terms_ref.at[(quarter, partner)[i] * group + group - 1],
            half_local.at[i],
        )

    if extra:
        inter_copy(group - 1).wait()
        for copy in swaps():
            copy.wait_recv()
        own_half = pl.ds(pl.multiple_of((quarter // 2) * 2 * rows, 16), 2 * rows)
        for i in range(2):
            inter_i = inter_x if i else inter_ref.at[group - 1]
            scale = (fock_in if i else fock_out)[0:1, :]
            left = jnp.dot(
                inter_i[own_half, :], whole[group - 1 + i], preferred_element_type=jnp.float32
            ).astype(jnp.bfloat16)
            projected = lax.dot_general(
                left, inter_i[...], (((1,), (1,)), ((), ())), preferred_element_type=jnp.float32
            )
            half_terms[i] = (scale * projected).astype(jnp.bfloat16)
            half_copy(i).start()
            half_own(i).start()

    def finish(c, carry):
        for d in range(1, quarters):
            term_arrival(c, d).wait_recv()
        for d in range(1, quarters):
            term_copy(c, d).wait_send()
        own_term(c).wait()
        return carry

    lax.fori_loop(0, full, finish, 0)
    if extra:
        for i in range(2):
            half_arrival(i).wait_recv()
            half_copy(i).wait_send()
            half_own(i).wait()
        for copy in swaps():
            copy.wait_send()
    for k in range(chunks):

        def sent(j, carry, k=k):
            owner_copy(k, (me + j) % holders).wait_send()
            return carry

        lax.fori_loop(1, holders, sent, 0)
        for d in range(1, quarters):
            peer_copy(k, d).wait_send()


def update_kernel(
    local_ref,
    gap_ref,
    terms_hbm,
    amp_hbm,
    integrals_hbm,
    energy_ref,
    new_hbm,
    residual_hbm,
    terms,
    amp,
    integrals,
    new,
    residual,
    columns,
    term_sem,
    in_sem,
    out_sem,
):
    quarter = lax.axis_index("dom")
    couplings = terms.shape[0]
    pair_count, rows, width = amp.shape

    def term_copy(c):
        return pltpu.make_async_copy(terms_hbm.at[c], terms.at[c], term_sem.at[c])

    def in_copies(p):
        return (
            pltpu.make_async_copy(amp_hbm.at[p], amp.at[p], in_sem.at[0, p]),
            pltpu.make_async_copy(integrals_hbm.at[p], integrals.at[p], in_sem.at[1, p]),
        )

    def out_copies(p):
        return (
            pltpu.make_async_copy(new.at[p], new_hbm.at[p], out_sem.at[0, p]),
            pltpu.make_async_copy(residual.at[p], residual_hbm.at[p], out_sem.at[1, p]),
        )

    def start_term(c, carry):
        term_copy(c).start()
        return carry

    for p in range(pair_count):
        for copy in in_copies(p):
            copy.start()
    lax.fori_loop(0, couplings, start_term, 0)
    columns[...] = jnp.transpose(energy_ref[...])
    own_rows = columns[pl.ds(pl.multiple_of(quarter * rows, 8), rows), :]

    def denominator(p):
        return own_rows[:, p : p + 1] + energy_ref[p : p + 1, :] + gap_ref[p]

    for p in range(pair_count):
        for copy in in_copies(p):
            copy.wait()
        current = amp[p].astype(jnp.float32)
        residual[p] = integrals[p].astype(jnp.float32) + denominator(p) * current

    def add_term(c, carry):
        term_copy(c).wait()
        p = local_ref[c]
        residual[p] = residual[p] - terms[c].astype(jnp.float32)
        return carry

    lax.fori_loop(0, couplings, add_term, 0)
    for p in range(pair_count):
        new[p] = amp[p].astype(jnp.float32) - residual[p] / denominator(p)
        for copy in out_copies(p):
            copy.start()
    for p in range(pair_count):
        for copy in out_copies(p):
            copy.wait()


def per_device(
    amplitude,
    integrals,
    virtual_energy,
    occupied_gap,
    pair_slot,
    coupling_source,
    coupling_target,
    coupling_fock,
    coupling_intersection,
):
    holders = lax.axis_size("pairs")
    quarters = lax.axis_size("dom")
    own_quarter = lax.axis_index("dom")
    pair_count, rows, width = amplitude.shape
    couplings = coupling_source.shape[0] // holders
    group = coupling_intersection.shape[0]
    slots = holders * SRC_CAP
    extra = 1 if quarters == 4 and group > 1 else 0
    chunk_rows = CHUNK_ROWS if rows % CHUNK_ROWS == 0 else rows
    chunks = rows // chunk_rows
    bf16 = jnp.bfloat16
    in_vmem = pl.BlockSpec(memory_space=VMEM)
    in_smem = pl.BlockSpec(memory_space=SMEM)
    anywhere = pl.BlockSpec(memory_space=pl.ANY)

    dma = pltpu.SemaphoreType.DMA
    terms, local = pl.pallas_call(
        functools.partial(exchange_kernel, holders, quarters),
        out_shape=(
            jax.ShapeDtypeStruct((couplings, rows, width), bf16),
            jax.ShapeDtypeStruct((couplings,), jnp.int32),
        ),
        in_specs=[in_smem, in_smem, in_smem, in_smem, anywhere, anywhere],
        out_specs=(anywhere, in_smem),
        scratch_shapes=[
            VMEM((slots, rows, width), bf16),
            VMEM((group, quarters * rows, width), bf16),
            SMEM((couplings,), jnp.int32),
            dma((group,)),
            VMEM((pair_count, rows, width), bf16),
            dma(()),
            VMEM((group + extra, quarters * rows, width), bf16),
            VMEM((quarters - 1, chunks, group + extra, chunk_rows, width), bf16),
            VMEM((group, quarters * rows, width), bf16),
            dma((chunks, holders)),
            dma((chunks, holders)),
            dma((chunks,)),
            dma((chunks, quarters)),
            dma((chunks, quarters)),
            dma((group, quarters)),
            dma((group, quarters)),
            dma((group,)),
            VMEM((quarters * rows, width), bf16),
            VMEM((8, width), jnp.float32),
            VMEM((8, width), jnp.float32),
            VMEM((2, 2 * rows, width), bf16),
            dma((2,)),
            dma((2,)),
            dma((2,)),
            dma((2,)),
            dma((2,)),
        ]
        + [VMEM((slots, chunk_rows, width), bf16)] * chunks,
        compiler_params=pltpu.CompilerParams(
            collective_id=0, has_side_effects=True, vmem_limit_bytes=60 << 20
        ),
        name="exchange",
    )(pair_slot, coupling_source, coupling_target, coupling_fock, amplitude, coupling_intersection)

    out = jax.ShapeDtypeStruct((pair_count, rows, width), jnp.float32)
    return pl.pallas_call(
        update_kernel,
        out_shape=(out, out),
        in_specs=[in_smem, in_smem, anywhere, anywhere, anywhere, in_vmem],
        out_specs=(anywhere, anywhere),
        scratch_shapes=[
            VMEM((couplings, rows, width), bf16),
            VMEM((pair_count, rows, width), bf16),
            VMEM((pair_count, rows, width), bf16),
            VMEM((pair_count, rows, width), jnp.float32),
            VMEM((pair_count, rows, width), jnp.float32),
            VMEM((width, pair_count), jnp.float32),
            dma((couplings,)),
            dma((2, pair_count)),
            dma((2, pair_count)),
        ],
        name="update",
    )(local, occupied_gap, terms, amplitude, integrals, virtual_energy)


def solution(mesh):
    in_specs = (
        P("pairs", "dom", None),
        P("pairs", "dom", None),
        P("pairs", None),
        P("pairs"),
        P(),
        P(),
        P(),
        P(("pairs", "dom")),
        P(("pairs", "dom"), None, None),
    )
    out_specs = (P("pairs", "dom", None), P("pairs", "dom", None))
    return jax.shard_map(
        per_device, mesh=mesh, in_specs=in_specs, out_specs=out_specs, check_vma=False
    )
```

profile of v0, /device:TPU:0, one launch (start us, length us, event | category | flops | bytes accessed | tf_op | source)
XLA Modules:
  0.0 58.2 jit_solution(530336316561434263)
XLA Ops:
  0.6 53.0 %exchange.1 = (bf16[16,96,384]{2,1,0:T(8,128)(2,1)}, s32[16]{0:T(128)}) custom-call(s32[64]{0:T(128)} %slot_ref.1, s32[128]{0:T(128)} %source_ref.1, s32[128]{0:T(128)} %target_ref.1, f32[4]{0:T(128)} %fock_ref.1, bf16[8,96,384]{2,1,0:T(8,128)(2,1)} %amp_hbm.3, bf16[4,384,384]{2,1,0:T(8,128)(2,1)} %inter_hbm.1), custom_call_target="tpu_custom_call" | custom-call | tf_op jit(solution)/shard_map/exchange/pallas_call | solution.py:482
  53.6 4.6 %update.1 = (f32[8,96,384]{2,1,0:T(8,128)}, f32[8,96,384]{2,1,0:T(8,128)}) custom-call(s32[16]{0:T(128)} %get-tuple-element.4.local_ref, f32[8]{0:T(128)} %gap_ref.1, bf16[16,96,384]{2,1,0:T(8,128)(2,1)} %get-tuple-element.5.terms_hbm, bf16[8,96,384]{2,1,0:T(8,128)(2,1)} %amp_hbm.3, bf16[8,96,384]{2,1,0:T(8,128)(2,1)} %integrals_hbm.1, f32[8,384]{1,0:T(8,128)} %energy_ref.1), custom_call_target="tpu_custom_call" | custom-call | tf_op jit(solution)/shard_map/update/pallas_call | solution.py:526
where the time goes:
time: 59 us; the launch traced here: 58.2 us
  Pallas kernels  57.5 us (97%)
  between operations  0.64 us (1%)
    pallas_call x1, Pallas kernels, per_device(): pl.pallas_call(functools.partial(exchange_kernel, holders, quarters), out...  53 us
    pallas_call x1, Pallas kernels, per_device(): pl.pallas_call(update_kernel, out_shape=(out, out), in_specs=[in_smem, in...  4.55 us

commit v1 on v0

--- a/solution.py
+++ b/solution.py
@@ -9,6 +9,7 @@
 
 SRC_CAP = 2
 CHUNK_ROWS = 16
+VMEM_ROOM = 48 << 20
 MESH = pl.DeviceIdType.MESH
 VMEM = pltpu.VMEM
 SMEM = pltpu.SMEM
@@ -378,6 +379,424 @@
             peer_copy(k, d).wait_send()
 
 
+def spread_kernel(
+    holders,
+    split,
+    slot_ref,
+    source_ref,
+    target_ref,
+    fock_ref,
+    amp_hbm,
+    inter_hbm,
+    terms_ref,
+    local_ref,
+    out_ref,
+    amp_ref,
+    amp_sem,
+    inter_ref,
+    inter_sem,
+    held_ref,
+    lead_ref,
+    rank_ref,
+    list_ref,
+    pair_rows,
+    full_terms,
+    half_terms,
+    fock_out,
+    fock_in,
+    send1,
+    recv1,
+    local1,
+    send2,
+    recv2,
+    swap_send,
+    swap_recv,
+    send3,
+    recv3,
+    local3,
+    half_send,
+    half_recv,
+    half_local,
+    *arrived,
+):
+    amp_copy = pltpu.make_async_copy(amp_hbm, amp_ref, amp_sem)
+    amp_copy.start()
+    me = lax.axis_index("pairs")
+    quarter = lax.axis_index("dom")
+    chunks = len(arrived)
+    slots, chunk_rows, width = arrived[0].shape
+    rows = chunk_rows * chunks
+    group = inter_hbm.shape[0]
+    distinct = pair_rows.shape[0]
+    half = holders // 2
+    my_half = me // half
+    in_half = me % half
+    sibling = quarter + 1 - 2 * (quarter % 2)
+    across = (quarter + 2) % 4
+    diagonal = sibling + 2 - 4 * (sibling // 2)
+    chip_start = pl.multiple_of((quarter // 2) * 2 * rows, 16)
+
+    barrier = pltpu.get_barrier_semaphore()
+
+    def greet(j, carry):
+        pl.semaphore_signal(
+            barrier, inc=1, device_id=((me + j) % holders, quarter), device_id_type=MESH
+        )
+        return carry
+
+    lax.fori_loop(1, holders, greet, 0)
+    for peer in (sibling, across, diagonal):
+        pl.semaphore_signal(barrier, inc=1, device_id=(me, peer), device_id_type=MESH)
+
+    def inter_copy(c):
+        return pltpu.make_async_copy(inter_hbm.at[c], inter_ref.at[c], inter_sem.at[c])
+
+    for c in range(group):
+        inter_copy(c).start()
+    for c in range(split):
+        fock_out[c] = jnp.full(fock_out.shape[1:], fock_ref[c], jnp.float32)
+
+    pair_count = amp_ref.shape[0]
+    couplings = source_ref.shape[0] // holders
+    base = me * pair_count
+    unroll = 8 if couplings % 8 == 0 else 1
+
+    def choose(h):
+        def block(i, ab):
+            first, second = ab
+            for u in range(unroll):
+                local = slot_ref[source_ref[h * couplings + i * unroll + u]] - base
+                mine = (local >= 0) & (local < pair_count)
+                free = first < 0
+                second = jnp.where(mine & jnp.logical_not(free) & (local != first), local, second)
+                first = jnp.where(mine & free, local, first)
+            return first, second
+
+        first, second = lax.fori_loop(
+            0, couplings // unroll, block, (jnp.int32(-1), jnp.int32(-1))
+        )
+        out_ref[h * SRC_CAP] = amp_ref[jnp.maximum(first, 0)]
+        out_ref[h * SRC_CAP + 1] = amp_ref[jnp.maximum(second, 0)]
+
+    def far_holder(j):
+        return (1 - my_half) * half + (in_half + j) % half
+
+    def near_holder(j):
+        return my_half * half + (in_half + j) % half
+
+    def choose_far(j, carry):
+        choose(far_holder(j))
+        return carry
+
+    def choose_near(j, carry):
+        choose(near_holder(j))
+        return carry
+
+    amp_copy.wait()
+    lax.fori_loop(0, half, choose_far, 0)
+    pl.semaphore_wait(barrier, holders - 1 + 3)
+
+    def owner_copy(k, h):
+        span = pl.ds(k * chunk_rows, chunk_rows)
+        return pltpu.make_async_remote_copy(
+            src_ref=out_ref.at[pl.ds(h * SRC_CAP, SRC_CAP), span],
+            dst_ref=arrived[k].at[pl.ds(me * SRC_CAP, SRC_CAP)],
+            send_sem=send1.at[k, h],
+            recv_sem=recv1.at[k, me],
+            device_id=(h, quarter),
+            device_id_type=MESH,
+        )
+
+    def arrival(k, h):
+        span = pl.ds(k * chunk_rows, chunk_rows)
+        return pltpu.make_async_remote_copy(
+            src_ref=out_ref.at[pl.ds(h * SRC_CAP, SRC_CAP), span],
+            dst_ref=arrived[k].at[pl.ds(h * SRC_CAP, SRC_CAP)],
+            send_sem=send1.at[k, h],
+            recv_sem=recv1.at[k, h],
+            device_id=(h, quarter),
+            device_id_type=MESH,
+        )
+
+    def own_copy(k):
+        span = pl.ds(k * chunk_rows, chunk_rows)
+        return pltpu.make_async_copy(
+            out_ref.at[pl.ds(me * SRC_CAP, SRC_CAP), span],
+            arrived[k].at[pl.ds(me * SRC_CAP, SRC_CAP)],
+            local1.at[k],
+        )
+
+    def send_far(k):
+        def far(j, carry):
+            owner_copy(k, far_holder(j)).start()
+            return carry
+
+        lax.fori_loop(0, half, far, 0)
+
+    def send_near(k):
+        def near(j, carry):
+            owner_copy(k, near_holder(j)).start()
+            return carry
+
+        lax.fori_loop(1, half, near, 0)
+        own_copy(k).start()
+
+    def swaps():
+        for c in range(split):
+            yield pltpu.make_async_remote_copy(
+                src_ref=inter_hbm.at[c],
+                dst_ref=inter_ref.at[group + c],
+                send_sem=swap_send.at[c],
+                recv_sem=swap_recv.at[c],
+                device_id=(me, across),
+                device_id_type=MESH,
+            )
+        yield pltpu.make_async_remote_copy(
+            src_ref=fock_out,
+            dst_ref=fock_in,
+            send_sem=swap_send.at[split],
+            recv_sem=swap_recv.at[split],
+            device_id=(me, across),
+            device_id_type=MESH,
+        )
+
+    send_far(0)
+    for copy in swaps():
+        copy.start()
+    lax.fori_loop(0, half, choose_near, 0)
+    send_near(0)
+    for k in range(1, chunks):
+        send_far(k)
+        send_near(k)
+
+    def own_step(c, count):
+        pair = source_ref[me * couplings + c]
+        slot = slot_ref[pair]
+        owner = lax.div(slot, jnp.int32(pair_count))
+
+        def block(i, carry):
+            first, lead = carry
+            for u in range(unroll):
+                at = couplings - 1 - (i * unroll + u)
+                other_pair = source_ref[me * couplings + at]
+                other = slot_ref[other_pair]
+                same = lax.div(other, jnp.int32(pair_count)) == owner
+                first = jnp.where(same, other, first)
+                lead = jnp.where(other_pair == pair, at, lead)
+            return first, lead
+
+        first, lead = lax.fori_loop(0, couplings // unroll, block, (slot, c))
+        held_ref[c] = owner * SRC_CAP + jnp.where(first == slot, 0, 1)
+        lead_ref[c] = lead
+        rank_ref[c] = count
+        local_ref[c] = slot_ref[target_ref[me * couplings + c]] - base
+        return count + jnp.where(lead == c, 1, 0)
+
+    lax.fori_loop(0, couplings, own_step, jnp.int32(0))
+
+    def list_step(j, carry):
+        def block(i, found):
+            for u in range(unroll):
+                c = i * unroll + u
+                found = jnp.where((lead_ref[c] == c) & (rank_ref[c] == j), held_ref[c], found)
+            return found
+
+        list_ref[j] = lax.fori_loop(0, couplings // unroll, block, jnp.int32(0))
+        return carry
+
+    lax.fori_loop(0, distinct, list_step, 0)
+
+    def span_of(owner, k):
+        start = pl.multiple_of(owner * rows + k * chunk_rows, 16)
+        return pair_rows.at[:, pl.ds(start, chunk_rows)]
+
+    def rows_copy(kind, k, owner, peer, landed):
+        return pltpu.make_async_remote_copy(
+            src_ref=span_of(owner, k),
+            dst_ref=span_of(landed, k),
+            send_sem=send2.at[kind, k],
+            recv_sem=recv2.at[kind, k],
+            device_id=(me, peer),
+            device_id_type=MESH,
+        )
+
+    def across_copy(k):
+        return rows_copy(0, k, quarter, across, quarter)
+
+    def across_arrival(k):
+        return rows_copy(0, k, quarter, across, across)
+
+    def sibling_copy(k):
+        return rows_copy(1, k, quarter, sibling, quarter)
+
+    def sibling_arrival(k):
+        return rows_copy(1, k, quarter, sibling, sibling)
+
+    def relay_copy(k):
+        return rows_copy(2, k, across, sibling, across)
+
+    def relay_arrival(k):
+        return rows_copy(2, k, across, sibling, diagonal)
+
+    def take_chunk(k):
+        def take(j, carry):
+            arrival(k, (me + j) % holders).wait_recv()
+            return carry
+
+        lax.fori_loop(1, holders, take, 0)
+        own_copy(k).wait()
+        start = pl.multiple_of(quarter * rows + k * chunk_rows, 16)
+
+        def pick(j, carry):
+            pair_rows[j, pl.ds(start, chunk_rows)] = arrived[k][list_ref[j]]
+            return carry
+
+        lax.fori_loop(0, distinct, pick, 0)
+        across_copy(k).start()
+        sibling_copy(k).start()
+
+    def relay_chunk(k):
+        across_arrival(k).wait_recv()
+        relay_copy(k).start()
+
+    relayed = 0
+    for k in range(chunks):
+        take_chunk(k)
+        if k >= 2:
+            relay_chunk(relayed)
+            relayed += 1
+    while relayed < chunks:
+        relay_chunk(relayed)
+        relayed += 1
+    for k in range(chunks):
+        sibling_arrival(k).wait_recv()
+        relay_arrival(k).wait_recv()
+
+    def source_of(owner, c):
+        return rank_ref[lead_ref[owner * group + c]]
+
+    def full_copy(c, peer, at):
+        return pltpu.make_async_remote_copy(
+            src_ref=full_terms.at[c, pl.ds(pl.multiple_of(peer * rows, 16), rows)],
+            dst_ref=terms_ref.at[quarter * group + split + c],
+            send_sem=send3.at[c, at],
+            recv_sem=recv3.at[c, at],
+            device_id=(me, peer),
+            device_id_type=MESH,
+        )
+
+    def full_arrival(c, peer, at):
+        return pltpu.make_async_remote_copy(
+            src_ref=full_terms.at[c, pl.ds(pl.multiple_of(peer * rows, 16), rows)],
+            dst_ref=terms_ref.at[peer * group + split + c],
+            send_sem=send3.at[c, at],
+            recv_sem=recv3.at[c, at],
+            device_id=(me, peer),
+            device_id_type=MESH,
+        )
+
+    def full_own(c):
+        return pltpu.make_async_copy(
+            full_terms.at[c, pl.ds(pl.multiple_of(quarter * rows, 16), rows)],
+            terms_ref.at[quarter * group + split + c],
+            local3.at[c],
+        )
+
+    peers = (across, diagonal, sibling)
+
+    for c in range(group):
+        inter_copy(c).wait()
+
+    def multiply(c, carry):
+        inter = inter_ref[split + c]
+        left = jnp.dot(
+            inter, pair_rows[source_of(quarter, split + c)], preferred_element_type=jnp.float32
+        ).astype(jnp.bfloat16)
+        projected = lax.dot_general(
+            left, inter, (((1,), (1,)), ((), ())), preferred_element_type=jnp.float32
+        )
+        full_terms[c] = (fock_ref[split + c] * projected).astype(jnp.bfloat16)
+        for at, peer in enumerate(peers):
+            full_copy(c, peer, at).start()
+        full_own(c).start()
+        return carry
+
+    lax.fori_loop(0, group - split, multiply, 0)
+
+    def half_copy(i, owner, c):
+        return pltpu.make_async_remote_copy(
+            src_ref=half_terms.at[i, pl.ds(pl.multiple_of((sibling % 2) * rows, 16), rows)],
+            dst_ref=terms_ref.at[owner * group + c],
+            send_sem=half_send.at[i],
+            recv_sem=half_recv.at[i],
+            device_id=(me, sibling),
+            device_id_type=MESH,
+        )
+
+    def half_own(i, owner, c):
+        return pltpu.make_async_copy(
+            half_terms.at[i, pl.ds(pl.multiple_of((quarter % 2) * rows, 16), rows)],
+            terms_ref.at[owner * group + c],
+            half_local.at[i],
+        )
+
+    own_rows = pl.ds(chip_start, 2 * rows)
+    for copy in swaps():
+        copy.wait_recv()
+    for side in range(2):
+
+        def multiply_half(c, carry, side=side):
+            owner = across if side else quarter
+            scale = fock_in[c, 0:1, :] if side else fock_ref[c]
+            inter = inter_ref.at[side * group + c]
+            left = jnp.dot(
+                inter[own_rows, :],
+                pair_rows[source_of(owner, c)],
+                preferred_element_type=jnp.float32,
+            ).astype(jnp.bfloat16)
+            projected = lax.dot_general(
+                left, inter[...], (((1,), (1,)), ((), ())), preferred_element_type=jnp.float32
+            )
+            half_terms[side * split + c] = (scale * projected).astype(jnp.bfloat16)
+            half_copy(side * split + c, owner, c).start()
+            half_own(side * split + c, owner, c).start()
+            return carry
+
+        lax.fori_loop(0, split, multiply_half, 0)
+
+    def finish(c, carry):
+        for at, peer in enumerate(peers):
+            full_arrival(c, peer, at).wait_recv()
+        for at, peer in enumerate(peers):
+            full_copy(c, peer, at).wait_send()
+        full_own(c).wait()
+        return carry
+
+    lax.fori_loop(0, group - split, finish, 0)
+    for side in range(2):
+
+        def finish_half(c, carry, side=side):
+            i = side * split + c
+            half_copy(i, diagonal if side else sibling, c).wait_recv()
+            half_copy(i, across if side else quarter, c).wait_send()
+            half_own(i, across if side else quarter, c).wait()
+            return carry
+
+        lax.fori_loop(0, split, finish_half, 0)
+    for copy in swaps():
+        copy.wait_send()
+    for k in range(chunks):
+
+        def sent(j, carry, k=k):
+            owner_copy(k, (me + j) % holders).wait_send()
+            return carry
+
+        lax.fori_loop(1, holders, sent, 0)
+        across_copy(k).wait_send()
+        sibling_copy(k).wait_send()
+        relay_copy(k).wait_send()
+
+
 def update_kernel(
     local_ref,
     gap_ref,
@@ -479,48 +898,103 @@
     anywhere = pl.BlockSpec(memory_space=pl.ANY)
 
     dma = pltpu.SemaphoreType.DMA
-    terms, local = pl.pallas_call(
-        functools.partial(exchange_kernel, holders, quarters),
-        out_shape=(
-            jax.ShapeDtypeStruct((couplings, rows, width), bf16),
-            jax.ShapeDtypeStruct((couplings,), jnp.int32),
-        ),
-        in_specs=[in_smem, in_smem, in_smem, in_smem, anywhere, anywhere],
-        out_specs=(anywhere, in_smem),
-        scratch_shapes=[
-            VMEM((slots, rows, width), bf16),
-            VMEM((group, quarters * rows, width), bf16),
-            SMEM((couplings,), jnp.int32),
-            dma((group,)),
-            VMEM((pair_count, rows, width), bf16),
-            dma(()),
-            VMEM((group + extra, quarters * rows, width), bf16),
-            VMEM((quarters - 1, chunks, group + extra, chunk_rows, width), bf16),
-            VMEM((group, quarters * rows, width), bf16),
-            dma((chunks, holders)),
-            dma((chunks, holders)),
-            dma((chunks,)),
-            dma((chunks, quarters)),
-            dma((chunks, quarters)),
-            dma((group, quarters)),
-            dma((group, quarters)),
-            dma((group,)),
-            VMEM((quarters * rows, width), bf16),
-            VMEM((8, width), jnp.float32),
-            VMEM((8, width), jnp.float32),
-            VMEM((2, 2 * rows, width), bf16),
-            dma((2,)),
-            dma((2,)),
-            dma((2,)),
-            dma((2,)),
-            dma((2,)),
-        ]
-        + [VMEM((slots, chunk_rows, width), bf16)] * chunks,
-        compiler_params=pltpu.CompilerParams(
-            collective_id=0, has_side_effects=True, vmem_limit_bytes=60 << 20
-        ),
-        name="exchange",
-    )(pair_slot, coupling_source, coupling_target, coupling_fock, amplitude, coupling_intersection)
+    distinct = couplings // 2
+    whole_rows = quarters * rows
+    held_rows = (
+        2 * slots
+        + pair_count
+        + quarters * (2 * group + distinct)
+        + 2 * group
+    ) * rows
+    fits = 2 * width * held_rows <= VMEM_ROOM
+    if quarters == 4 and group >= 2 and group % 2 == 0 and holders % 2 == 0 and fits:
+        split = group // 2
+        terms, local = pl.pallas_call(
+            functools.partial(spread_kernel, holders, split),
+            out_shape=(
+                jax.ShapeDtypeStruct((couplings, rows, width), bf16),
+                jax.ShapeDtypeStruct((couplings,), jnp.int32),
+            ),
+            in_specs=[in_smem, in_smem, in_smem, in_smem, anywhere, anywhere],
+            out_specs=(anywhere, in_smem),
+            scratch_shapes=[
+                VMEM((slots, rows, width), bf16),
+                VMEM((pair_count, rows, width), bf16),
+                dma(()),
+                VMEM((group + split, whole_rows, width), bf16),
+                dma((group,)),
+                SMEM((couplings,), jnp.int32),
+                SMEM((couplings,), jnp.int32),
+                SMEM((couplings,), jnp.int32),
+                SMEM((distinct,), jnp.int32),
+                VMEM((distinct, whole_rows, width), bf16),
+                VMEM((group - split, whole_rows, width), bf16),
+                VMEM((2 * split, 2 * rows, width), bf16),
+                VMEM((split, 8, width), jnp.float32),
+                VMEM((split, 8, width), jnp.float32),
+                dma((chunks, holders)),
+                dma((chunks, holders)),
+                dma((chunks,)),
+                dma((3, chunks)),
+                dma((3, chunks)),
+                dma((split + 1,)),
+                dma((split + 1,)),
+                dma((group - split, 3)),
+                dma((group - split, 3)),
+                dma((group - split,)),
+                dma((2 * split,)),
+                dma((2 * split,)),
+                dma((2 * split,)),
+            ]
+            + [VMEM((slots, chunk_rows, width), bf16)] * chunks,
+            compiler_params=pltpu.CompilerParams(
+                collective_id=0, has_side_effects=True, vmem_limit_bytes=60 << 20
+            ),
+            name="exchange",
+        )(pair_slot, coupling_source, coupling_target, coupling_fock, amplitude, coupling_intersection)
+    else:
+        terms, local = pl.pallas_call(
+            functools.partial(exchange_kernel, holders, quarters),
+            out_shape=(
+                jax.ShapeDtypeStruct((couplings, rows, width), bf16),
+                jax.ShapeDtypeStruct((couplings,), jnp.int32),
+            ),
+            in_specs=[in_smem, in_smem, in_smem, in_smem, anywhere, anywhere],
+            out_specs=(anywhere, in_smem),
+            scratch_shapes=[
+                VMEM((slots, rows, width), bf16),
+                VMEM((group, quarters * rows, width), bf16),
+                SMEM((couplings,), jnp.int32),
+                dma((group,)),
+                VMEM((pair_count, rows, width), bf16),
+                dma(()),
+                VMEM((group + extra, quarters * rows, width), bf16),
+                VMEM((quarters - 1, chunks, group + extra, chunk_rows, width), bf16),
+                VMEM((group, quarters * rows, width), bf16),
+                dma((chunks, holders)),
+                dma((chunks, holders)),
+                dma((chunks,)),
+                dma((chunks, quarters)),
+                dma((chunks, quarters)),
+                dma((group, quarters)),
+                dma((group, quarters)),
+                dma((group,)),
+                VMEM((quarters * rows, width), bf16),
+                VMEM((8, width), jnp.float32),
+                VMEM((8, width), jnp.float32),
+                VMEM((2, 2 * rows, width), bf16),
+                dma((2,)),
+                dma((2,)),
+                dma((2,)),
+                dma((2,)),
+                dma((2,)),
+            ]
+            + [VMEM((slots, chunk_rows, width), bf16)] * chunks,
+            compiler_params=pltpu.CompilerParams(
+                collective_id=0, has_side_effects=True, vmem_limit_bytes=60 << 20
+            ),
+            name="exchange",
+        )(pair_slot, coupling_source, coupling_target, coupling_fock, amplitude, coupling_intersection)
 
     out = jax.ShapeDtypeStruct((pair_count, rows, width), jnp.float32)
     return pl.pallas_call(

time: 59 us -> 55.6 us (0.942); the launches traced: 58.2 us -> 55.4 us
  Pallas kernels: 57.5 us -> 54.7 us
    pallas_call x1, Pallas kernels: 53 us -> 50.2 us  [per_device(): pl.pallas_call(functools.partial(spread_kernel, holders, split), out_shap...]
where the time goes in v1:
time: 55.6 us; the launch traced here: 55.4 us
  Pallas kernels  54.7 us (98%)
  between operations  0.64 us (1%)
    pallas_call x1, Pallas kernels, per_device(): pl.pallas_call(functools.partial(spread_kernel, holders, split), out_shap...  50.2 us
    pallas_call x1, Pallas kernels, per_device(): pl.pallas_call(update_kernel, out_shape=(out, out), in_specs=[in_smem, in...  4.55 us

profile of v1, /device:TPU:0, one launch (start us, length us, event | category | flops | bytes accessed | tf_op | source)
XLA Modules:
  0.0 55.4 jit_solution(18320820524148138761)
XLA Ops:
  0.6 50.2 %exchange.1 = (bf16[16,96,384]{2,1,0:T(8,128)(2,1)}, s32[16]{0:T(128)}) custom-call(s32[64]{0:T(128)} %slot_ref.1, s32[128]{0:T(128)} %source_ref.1, s32[128]{0:T(128)} %target_ref.1, f32[4]{0:T(128)} %fock_ref.1, bf16[8,96,384]{2,1,0:T(8,128)(2,1)} %amp_hbm.3, bf16[4,384,384]{2,1,0:T(8,128)(2,1)} %inter_hbm.1), custom_call_target="tpu_custom_call" | custom-call | tf_op jit(solution)/shard_map/exchange/pallas_call | solution.py:912
  50.8 4.6 %update.1 = (f32[8,96,384]{2,1,0:T(8,128)}, f32[8,96,384]{2,1,0:T(8,128)}) custom-call(s32[16]{0:T(128)} %get-tuple-element.4.local_ref, f32[8]{0:T(128)} %gap_ref.1, bf16[16,96,384]{2,1,0:T(8,128)(2,1)} %get-tuple-element.5.terms_hbm, bf16[8,96,384]{2,1,0:T(8,128)(2,1)} %amp_hbm.3, bf16[8,96,384]{2,1,0:T(8,128)(2,1)} %integrals_hbm.1, f32[8,384]{1,0:T(8,128)} %energy_ref.1), custom_call_target="tpu_custom_call" | custom-call | tf_op jit(solution)/shard_map/update/pallas_call | solution.py:1000
